TPU v7x, 32 devices: a whole 2x2x4 slice. The times are simulated.
32 devices in a mesh: heads: 8 (over y, x, core), batch: 4 (over z).
Axes of the slice: x: 2, y: 2, z: 4, core: 2. Of those that a mesh axis runs over, the one named last changes fastest.
Arguments:
- tokens: bfloat16 [2, 4, 1024, 2048], P(None, 'batch', 'heads'), may hold values from -6 to 6
- cotangent: bfloat16 [2, 4, 1024, 2048], P(None, 'batch', 'heads'), may hold values from -6 to 6
- doc_lengths: int32 [2, 4, 4], P(None, 'batch'), may hold values from 1 to 768, 1024 in all within a row
- pad_mask: int32 [2, 4, 1024], P(None, 'batch'), may hold values 0 or 1
- w_query: bfloat16 [2048, 1024], P(None, 'heads'), may hold values from -0.1875 to 0.1875
- w_key: bfloat16 [2048, 1024], P(None, 'heads'), may hold values from -0.1875 to 0.1875
- w_value: bfloat16 [2048, 1024], P(None, 'heads'), may hold values from -0.125 to 0.125
- w_out: bfloat16 [1024, 2048], P('heads'), may hold values from -0.75 to 0.75
- w_gate: bfloat16 [2048, 8192], P(None, 'heads'), may hold values from -0.125 to 0.125
- w_up: bfloat16 [2048, 8192], P(None, 'heads'), may hold values from -0.125 to 0.125
- w_down: bfloat16 [8192, 2048], P('heads'), may hold values from -0.0625 to 0.0625
- norm_attn: float32 [2048], replicated, may hold values from 0.1 to 1.9
- norm_mlp: float32 [2048], replicated, may hold values from 0.1 to 1.9
- mix_gate: float32 [8], P('heads'), may hold values from -2 to 2
Outputs:
- layer_out: bfloat16 [2, 4, 1024, 2048], P(None, 'batch', 'heads')
- grad_tokens: float32 [2, 4, 1024, 2048], P(None, 'batch', 'heads')
- grad_w_query: float32 [2048, 1024], P(None, 'heads')
- grad_w_key: float32 [2048, 1024], P(None, 'heads')
- grad_w_value: float32 [2048, 1024], P(None, 'heads')
- grad_w_out: float32 [1024, 2048], P('heads')
- grad_w_gate: float32 [2048, 8192], P(None, 'heads')
- grad_w_up: float32 [2048, 8192], P(None, 'heads')
- grad_w_down: float32 [8192, 2048], P('heads')
- grad_norm_attn: float32 [2048], replicated
- grad_norm_mlp: float32 [2048], replicated
- grad_mix_gate: float32 [8], P('heads')
Inputs may be any that keep to these rules, and one draw needn't show every extreme that they name: `doc_lengths`: the 4 lengths of a sequence sum to 1024; the longest is 768.
All inputs are finite; a program needn't handle non-finite values. No bound on the sum of `pad_mask` on one device may be relied on, other than what follows from the above.
Results may differ from a plain program's by a relative error of at most 0.018.
Values may be sent and summed in bfloat16 or wider, within the bound.
No kernel may reach another device: no remote copies, remote signals or barrier semaphores. Data moves between devices by JAX's collectives and lax.ppermute only.
A program may use at most 256 MiB of HBM per device.

v0:
```python
import jax
import jax.numpy as jnp
from jax import lax
from jax.sharding import PartitionSpec as P

DH = 128
SEG = 512
SEGS = 2
LEN = 1024
MICRO = 2
epsilon = 1e-05
big_negative = -1e30


def dot_rows(left_mat, right_mat):
    return lax.dot_general(
        left_mat, right_mat, (((1,), (1,)), ((), ())), preferred_element_type=jnp.float32
    )


def dot_cols(left_mat, right_mat):
    return lax.dot_general(
        left_mat, right_mat, (((0,), (0,)), ((), ())), preferred_element_type=jnp.float32
    )


def norm_rows(row_block, gain_vec):
    row_scale = lax.rsqrt(jnp.mean(row_block * row_block, axis=-1, keepdims=True) + epsilon)
    return (row_block * row_scale * gain_vec, row_scale)


def norm_back(row_block, row_scale, gain_vec, upstream):
    shaped = upstream * gain_vec
    inner = jnp.mean(shaped * row_block, axis=-1, keepdims=True)
    d_rows = row_scale * shaped - row_block * row_scale * row_scale * row_scale * inner
    d_gain = jnp.sum(upstream * row_block * row_scale, axis=0)
    return (d_rows, d_gain)


def positive(values_in):
    return jnp.where(values_in > 0, values_in + 1.0, jnp.exp(values_in))


def local_mask(begin_row, positions, doc_ids, valid_keys):
    seg_pos = positions[begin_row : begin_row + SEG]
    seg_doc = doc_ids[begin_row : begin_row + SEG]
    seg_valid = valid_keys[begin_row : begin_row + SEG]
    same_doc = seg_doc[:, None] == seg_doc[None, :]
    causal = seg_pos[None, :] <= seg_pos[:, None]
    return same_doc & causal & (seg_valid[None, :] | (seg_pos[None, :] == seg_pos[:, None]))


def memory_mask(begin_row, doc_ids, valid_keys):
    seg_doc = doc_ids[begin_row : begin_row + SEG]
    return (seg_doc[:, None] == doc_ids[None, :begin_row]) & valid_keys[None, :begin_row]


def head_forward(query_all, key_all, value_all, share, positions, doc_ids, valid_keys):
    score_scale = DH ** (-0.5)
    pos_query = positive(query_all.astype(jnp.float32)).astype(jnp.bfloat16)
    pos_key = positive(key_all.astype(jnp.float32)).astype(jnp.bfloat16)
    dotted_parts, recalled_parts, total_parts = ([], [], [])
    for segment in range(SEGS):
        begin_row = segment * SEG
        query_seg = query_all[begin_row : begin_row + SEG]
        key_seg = key_all[begin_row : begin_row + SEG]
        value_seg = value_all[begin_row : begin_row + SEG]
        allowed = local_mask(begin_row, positions, doc_ids, valid_keys)
        scores = jnp.where(allowed, dot_rows(query_seg, key_seg) * score_scale, big_negative)
        row_top = jnp.max(scores, axis=1, keepdims=True)
        log_total = row_top + jnp.log(jnp.sum(jnp.exp(scores - row_top), axis=1, keepdims=True))
        soft_probs = jnp.exp(scores - log_total)
        dotted_parts.append(
            jnp.dot(soft_probs.astype(jnp.bfloat16), value_seg, preferred_element_type=jnp.float32)
        )
        total_parts.append(log_total)
        if segment == 0:
            recalled_parts.append(jnp.zeros((SEG, DH), jnp.float32))
        else:
            mem_allowed = memory_mask(begin_row, doc_ids, valid_keys)
            weights = jnp.where(
                mem_allowed,
                dot_rows(pos_query[begin_row : begin_row + SEG], pos_key[:begin_row]),
                0.0,
            )
            denominator = jnp.maximum(jnp.sum(weights, axis=1, keepdims=True), 1.0)
            numerator = jnp.dot(
                weights.astype(jnp.bfloat16),
                value_all[:begin_row],
                preferred_element_type=jnp.float32,
            )
            recalled_parts.append(numerator / denominator)
    dotted = jnp.concatenate(dotted_parts, axis=0)
    recalled = jnp.concatenate(recalled_parts, axis=0)
    mixed_head = share * recalled + (1.0 - share) * dotted
    return (mixed_head, dotted, recalled, jnp.concatenate(total_parts, axis=0))


def head_backward(
    query_all,
    key_all,
    value_all,
    share,
    positions,
    doc_ids,
    valid_keys,
    d_mixed,
    dotted,
    recalled,
    log_totals,
):
    score_scale = DH ** (-0.5)
    query_float = query_all.astype(jnp.float32)
    key_float = key_all.astype(jnp.float32)
    pos_query = positive(query_float).astype(jnp.bfloat16)
    pos_key = positive(key_float).astype(jnp.bfloat16)
    d_share = jnp.sum(d_mixed * (recalled - dotted)) * share * (1.0 - share)
    d_dotted = ((1.0 - share) * d_mixed).astype(jnp.bfloat16)
    d_recalled = share * d_mixed
    zeros_block = jnp.zeros((LEN, DH), jnp.float32)
    d_query, d_key, d_value, d_posq, d_posk = (
        zeros_block,
        zeros_block,
        zeros_block,
        zeros_block,
        zeros_block,
    )
    for segment in range(SEGS):
        begin_row = segment * SEG
        end_row = begin_row + SEG
        query_seg = query_all[begin_row:end_row]
        key_seg = key_all[begin_row:end_row]
        value_seg = value_all[begin_row:end_row]
        allowed = local_mask(begin_row, positions, doc_ids, valid_keys)
        scores = jnp.where(allowed, dot_rows(query_seg, key_seg) * score_scale, big_negative)
        soft_probs = jnp.exp(scores - log_totals[begin_row:end_row])
        d_dot_seg = d_dotted[begin_row:end_row]
        d_value = d_value.at[begin_row:end_row].add(
            dot_cols(soft_probs.astype(jnp.bfloat16), d_dot_seg)
        )
        d_probs = dot_rows(d_dot_seg, value_seg)
        d_scores = (
            soft_probs * (d_probs - jnp.sum(soft_probs * d_probs, axis=1, keepdims=True))
        ).astype(jnp.bfloat16)
        d_query = d_query.at[begin_row:end_row].add(
            jnp.dot(d_scores, key_seg, preferred_element_type=jnp.float32) * score_scale
        )
        d_key = d_key.at[begin_row:end_row].add(dot_cols(d_scores, query_seg) * score_scale)
        if segment > 0:
            posq_seg = pos_query[begin_row:end_row]
            posk_prev = pos_key[:begin_row]
            value_prev = value_all[:begin_row]
            mem_allowed = memory_mask(begin_row, doc_ids, valid_keys)
            weights = jnp.where(mem_allowed, dot_rows(posq_seg, posk_prev), 0.0)
            row_total = jnp.sum(weights, axis=1, keepdims=True)
            denominator = jnp.maximum(row_total, 1.0)
            weights_low = weights.astype(jnp.bfloat16)
            numerator = jnp.dot(weights_low, value_prev, preferred_element_type=jnp.float32)
            d_recall_seg = d_recalled[begin_row:end_row]
            d_numer = (d_recall_seg / denominator).astype(jnp.bfloat16)
            d_denom = jnp.where(
                row_total > 1.0,
                -jnp.sum(d_recall_seg * numerator, axis=1, keepdims=True)
                / (denominator * denominator),
                0.0,
            )
            d_weights = jnp.where(mem_allowed, dot_rows(d_numer, value_prev) + d_denom, 0.0).astype(
                jnp.bfloat16
            )
            d_posq = d_posq.at[begin_row:end_row].add(
                jnp.dot(d_weights, posk_prev, preferred_element_type=jnp.float32)
            )
            d_posk = d_posk.at[:begin_row].add(dot_cols(d_weights, posq_seg))
            d_value = d_value.at[:begin_row].add(dot_cols(weights_low, d_numer))
    d_query = d_query + d_posq * jnp.where(query_float > 0, 1.0, jnp.exp(query_float))
    d_key = d_key + d_posk * jnp.where(key_float > 0, 1.0, jnp.exp(key_float))
    return (
        d_query.astype(jnp.bfloat16),
        d_key.astype(jnp.bfloat16),
        d_value.astype(jnp.bfloat16),
        d_share,
    )


def per_device(
    tokens,
    cotangent,
    doc_lengths,
    pad_mask,
    w_query,
    w_key,
    w_value,
    w_out,
    w_gate,
    w_up,
    w_down,
    norm_attn,
    norm_mlp,
    mix_gate,
):
    local_width = w_query.shape[1]
    hidden_cols = w_gate.shape[1]
    w_qkv = jnp.concatenate([w_query, w_key, w_value], axis=1)
    w_gate_up = jnp.concatenate([w_gate, w_up], axis=1)
    shares = jax.nn.sigmoid(mix_gate)
    positions = jnp.arange(LEN, dtype=jnp.int32)
    grad_qkv = jnp.zeros(w_qkv.shape, jnp.float32)
    grad_out = jnp.zeros(w_out.shape, jnp.float32)
    grad_gate_up = jnp.zeros(w_gate_up.shape, jnp.float32)
    grad_down = jnp.zeros(w_down.shape, jnp.float32)
    grad_mix = jnp.zeros(mix_gate.shape, jnp.float32)
    grad_gain_attn = jnp.zeros(norm_attn.shape, jnp.float32)
    grad_gain_mlp = jnp.zeros(norm_mlp.shape, jnp.float32)
    out_list, grad_in_list = ([], [])
    for micro_step in range(MICRO):
        doc_ends = jnp.cumsum(doc_lengths[micro_step, 0])
        doc_ids = jnp.sum((positions[:, None] >= doc_ends[None, :]).astype(jnp.int32), axis=1)
        valid_keys = pad_mask[micro_step, 0] == 1
        x_rows = tokens[micro_step, 0].astype(jnp.float32)
        normed_attn, scale_attn = norm_rows(x_rows, norm_attn)
        low_attn = normed_attn.astype(jnp.bfloat16)
        full_attn = lax.all_gather(low_attn, "heads", axis=0, tiled=True)
        qkv_all = jnp.dot(full_attn, w_qkv, preferred_element_type=jnp.float32).astype(jnp.bfloat16)
        head_inputs, head_kept, mixed_parts = ([], [], [])
        head_index = 0
        col_begin = head_index * DH
        query_all = qkv_all[:, col_begin : col_begin + DH]
        key_all = qkv_all[:, local_width + col_begin : local_width + col_begin + DH]
        value_all = qkv_all[:, 2 * local_width + col_begin : 2 * local_width + col_begin + DH]
        result_head = head_forward(
            query_all, key_all, value_all, shares[head_index], positions, doc_ids, valid_keys
        )
        head_inputs.append((query_all, key_all, value_all))
        head_kept.append(result_head)
        mixed_parts.append(result_head[0])
        mixed_low = mixed_parts[0].astype(jnp.bfloat16)
        attn_rows = lax.psum_scatter(
            jnp.dot(mixed_low, w_out, preferred_element_type=jnp.float32),
            "heads",
            scatter_dimension=0,
            tiled=True,
        )
        mid_rows = x_rows + attn_rows
        normed_mlp, scale_mlp = norm_rows(mid_rows, norm_mlp)
        low_mlp = normed_mlp.astype(jnp.bfloat16)
        full_mlp = lax.all_gather(low_mlp, "heads", axis=0, tiled=True)
        gate_up = jnp.dot(full_mlp, w_gate_up, preferred_element_type=jnp.float32)
        gate_pre = gate_up[:, :hidden_cols]
        up_pre = gate_up[:, hidden_cols:]
        sig_gate = jax.nn.sigmoid(gate_pre)
        hidden = (gate_pre * sig_gate * up_pre).astype(jnp.bfloat16)
        mlp_rows = lax.psum_scatter(
            jnp.dot(hidden, w_down, preferred_element_type=jnp.float32).astype(jnp.bfloat16),
            "heads",
            scatter_dimension=0,
            tiled=True,
        ).astype(jnp.float32)
        out_list.append((mid_rows + mlp_rows).astype(jnp.bfloat16))
        cot_low = cotangent[micro_step, 0]
        cot_full = lax.all_gather(cot_low, "heads", axis=0, tiled=True)
        grad_down = grad_down + dot_cols(hidden, cot_full)
        d_hidden = dot_rows(cot_full, w_down)
        d_up = d_hidden * gate_pre * sig_gate
        d_gate = d_hidden * up_pre * sig_gate * (1.0 + gate_pre * (1.0 - sig_gate))
        d_gate_up = jnp.concatenate([d_gate, d_up], axis=1).astype(jnp.bfloat16)
        grad_gate_up = grad_gate_up + dot_cols(full_mlp, d_gate_up)
        d_norm_mlp = lax.psum_scatter(
            dot_rows(d_gate_up, w_gate_up), "heads", scatter_dimension=0, tiled=True
        )
        d_mid_norm, gain_mlp_part = norm_back(mid_rows, scale_mlp, norm_mlp, d_norm_mlp)
        grad_gain_mlp = grad_gain_mlp + gain_mlp_part
        d_mid = d_mid_norm + cot_low.astype(jnp.float32)
        d_attn_full = lax.all_gather(d_mid.astype(jnp.bfloat16), "heads", axis=0, tiled=True)
        grad_out = grad_out + dot_cols(mixed_low, d_attn_full)
        d_mixed_all = dot_rows(d_attn_full, w_out)
        dq_parts, dk_parts, dv_parts, dshare_parts = ([], [], [], [])
        head_index = 0
        col_begin = head_index * DH
        query_all, key_all, value_all = head_inputs[head_index]
        kept_head = head_kept[head_index]
        back_head = head_backward(
            query_all,
            key_all,
            value_all,
            shares[head_index],
            positions,
            doc_ids,
            valid_keys,
            d_mixed_all,
            kept_head[1],
            kept_head[2],
            kept_head[3],
        )
        dq_parts.append(back_head[0])
        dk_parts.append(back_head[1])
        dv_parts.append(back_head[2])
        dshare_parts.append(back_head[3])
        grad_mix = grad_mix + jnp.stack(dshare_parts)
        d_qkv = jnp.concatenate(dq_parts + dk_parts + dv_parts, axis=1)
        grad_qkv = grad_qkv + dot_cols(full_attn, d_qkv)
        d_norm_attn = lax.psum_scatter(
            dot_rows(d_qkv, w_qkv).astype(jnp.bfloat16), "heads", scatter_dimension=0, tiled=True
        ).astype(jnp.float32)
        d_x_norm, gain_attn_part = norm_back(x_rows, scale_attn, norm_attn, d_norm_attn)
        grad_gain_attn = grad_gain_attn + gain_attn_part
        grad_in_list.append(d_x_norm + d_mid)
    grad_qkv, grad_out, grad_gate_up, grad_down, grad_mix = (
        lax.psum(grad_qkv.astype(jnp.bfloat16), "batch").astype(jnp.float32),
        lax.psum(grad_out.astype(jnp.bfloat16), "batch").astype(jnp.float32),
        lax.psum(grad_gate_up.astype(jnp.bfloat16), "batch").astype(jnp.float32),
        lax.psum(grad_down.astype(jnp.bfloat16), "batch").astype(jnp.float32),
        lax.psum(grad_mix.astype(jnp.bfloat16), "batch").astype(jnp.float32),
    )
    grad_gain_attn, grad_gain_mlp = lax.psum((grad_gain_attn, grad_gain_mlp), ("heads", "batch"))
    layer_out = jnp.stack(out_list)[:, None]
    grad_tokens = jnp.stack(grad_in_list)[:, None]
    return (
        layer_out,
        grad_tokens,
        grad_qkv[:, :local_width],
        grad_qkv[:, local_width : 2 * local_width],
        grad_qkv[:, 2 * local_width :],
        grad_out,
        grad_gate_up[:, :hidden_cols],
        grad_gate_up[:, hidden_cols:],
        grad_down,
        grad_gain_attn,
        grad_gain_mlp,
        grad_mix,
    )


def solution(mesh):
    in_specs = (
        P(None, "batch", "heads", None),
        P(None, "batch", "heads", None),
        P(None, "batch", None),
        P(None, "batch", None),
        P(None, "heads"),
        P(None, "heads"),
        P(None, "heads"),
        P("heads", None),
        P(None, "heads"),
        P(None, "heads"),
        P("heads", None),
        P(),
        P(),
        P("heads"),
    )
    out_specs = (
        P(None, "batch", "heads", None),
        P(None, "batch", "heads", None),
        P(None, "heads"),
        P(None, "heads"),
        P(None, "heads"),
        P("heads", None),
        P(None, "heads"),
        P(None, "heads"),
        P("heads", None),
        P(),
        P(),
        P("heads"),
    )
    return jax.shard_map(
        per_device, mesh=mesh, in_specs=in_specs, out_specs=out_specs, check_vma=False
    )
```

profile of v0, /device:TPU:0, one launch (start us, length us, event | category | flops | bytes accessed | tf_op | source)
XLA Modules:
  0.0 1430.8 jit_solution(2356076530199268857)
XLA Ops:
  16.6 35.0 %all-gather.15.cloned.1.call-done = bf16[1024,2048]{1,0:T(8,128)(2,1)} async-done(((bf16[128,2048]{1,0:T(8,128)(2,1)}), bf16[1024,2048]{1,0:T(8,128)(2,1)}) %all-gather.15.cloned.1.call-update) | async-done | bytes 4194320 | tf_op jit(solution)/shard_map/all_gather | solution.py:222
  68.3 22.5 %all-gather.11.cloned.1.call-done = bf16[1024,2048]{1,0:T(8,128)(2,1)} async-done(((bf16[128,2048]{1,0:T(8,128)(2,1)}), bf16[1024,2048]{1,0:T(8,128)(2,1)}) %all-gather.11.cloned.1.call-update) | async-done | bytes 4194320 | tf_op jit(solution)/shard_map/all_gather | solution.py:222
  108.1 58.1 %reduce-scatter.13.cloned.1.call-done = f32[128,2048]{1,0:T(8,128)} async-done(((f32[1024,2048]{1,0:T(8,128)}), f32[128,2048]{1,0:T(8,128)}) %reduce-scatter.13.cloned.1.call-update) | async-done | bytes 1048592 | tf_op jit(solution)/shard_map/reduce_scatter | solution.py:237
  166.2 75.6 %reduce-scatter.9.cloned.1.call-done = f32[128,2048]{1,0:T(8,128)} async-done(((f32[1024,2048]{1,0:T(8,128)}), f32[128,2048]{1,0:T(8,128)}) %reduce-scatter.9.cloned.1.call-update) | async-done | bytes 1048592 | tf_op jit(solution)/shard_map/reduce_scatter | solution.py:237
  255.3 27.2 %all-gather.13.cloned.1.call-done = bf16[1024,2048]{1,0:T(8,128)(2,1)} async-done(((bf16[128,2048]{1,0:T(8,128)(2,1)}), bf16[1024,2048]{1,0:T(8,128)(2,1)}) %all-gather.13.cloned.1.call-update) | async-done | bytes 4194320 | tf_op jit(solution)/shard_map/all_gather | solution.py:246
  282.4 14.9 %fusion.167 = f32[1024,2048]{1,0:T(8,128)} fusion(bf16[1024,2048]{1,0:T(8,128)(2,1)} %all-gather.13.cloned.1.call-done, bf16[2048,2048]{1,0:T(8,128)(2,1)} %constant_dynamic-update-slice_fusion.3), kind=kOutput, calls=%fused_computation.320 | convolution fusion | flops 8589934592 | bytes 20971520 | tf_op jit(solution)/shard_map/dot_general | solution.py:247
  297.3 24.2 %all-gather.23.cloned.1.call-done = bf16[1,1,1024,2048]{3,2,1,0:T(8,128)(2,1)} async-done(((bf16[1,1,128,2048]{3,2,1,0:T(8,128)(2,1)}), bf16[1,1,1024,2048]{3,2,1,0:T(8,128)(2,1)}) %all-gather.23.cloned.1.call-update) | async-done | bytes 4194320 | tf_op jit(solution)/shard_map/all_gather | solution.py:260
  321.5 13.2 multiply_convert_fusion.3
  336.7 13.3 fusion.12
  350.1 71.3 %reduce-scatter.17.cloned.1.call-done = f32[128,2048]{1,0:T(8,128)} async-done(((f32[1024,2048]{1,0:T(8,128)}), f32[128,2048]{1,0:T(8,128)}) %reduce-scatter.17.cloned.1.call-update) | async-done | bytes 1048592 | tf_op jit(solution)/shard_map/reduce_scatter | solution.py:267
  425.2 36.1 %all-gather.17.cloned.1.call-done = bf16[1024,2048]{1,0:T(8,128)(2,1)} async-done(((bf16[128,2048]{1,0:T(8,128)(2,1)}), bf16[1024,2048]{1,0:T(8,128)(2,1)}) %all-gather.17.cloned.1.call-update) | async-done | bytes 4194320 | tf_op jit(solution)/shard_map/all_gather | solution.py:246
  461.3 14.6 %fusion.169 = f32[1024,2048]{1,0:T(8,128)} fusion(bf16[1024,2048]{1,0:T(8,128)(2,1)} %all-gather.17.cloned.1.call-done, bf16[2048,2048]{1,0:T(8,128)(2,1)} %constant_dynamic-update-slice_fusion.3), kind=kOutput, calls=%fused_computation.322 | convolution fusion | flops 8589934592 | bytes 20971520 | tf_op jit(solution)/shard_map/dot_general | solution.py:247
  475.9 24.7 %all-gather.25.cloned.1.call-done = bf16[1,1,1024,2048]{3,2,1,0:T(8,128)(2,1)} async-done(((bf16[1,1,128,2048]{3,2,1,0:T(8,128)(2,1)}), bf16[1,1,1024,2048]{3,2,1,0:T(8,128)(2,1)}) %all-gather.25.cloned.1.call-update) | async-done | bytes 4194320 | tf_op jit(solution)/shard_map/all_gather | solution.py:260
  500.7 13.2 multiply_convert_fusion.1
  516.0 13.3 fusion.10
  529.8 9.7 convolution_convert_fusion.3
  539.6 10.4 convolution_convert_fusion.2
  550.1 50.7 %reduce-scatter.21.cloned.1.call-done = f32[128,2048]{1,0:T(8,128)} async-done(((f32[1024,2048]{1,0:T(8,128)}), f32[128,2048]{1,0:T(8,128)}) %reduce-scatter.21.cloned.1.call-update) | async-done | bytes 1048592 | tf_op jit(solution)/shard_map/reduce_scatter | solution.py:267
  602.3 53.8 %reduce-scatter.11.cloned.1.call-done = bf16[128,2048]{1,0:T(8,128)(2,1)} async-done(((bf16[1024,2048]{1,0:T(8,128)(2,1)}), bf16[128,2048]{1,0:T(8,128)(2,1)}) %reduce-scatter.11.cloned.1.call-update) | async-done | bytes 524304 | tf_op jit(solution)/shard_map/reduce_scatter | solution.py:252
  656.1 55.5 %reduce-scatter.15.cloned.1.call-done = bf16[128,2048]{1,0:T(8,128)(2,1)} async-done(((bf16[1024,2048]{1,0:T(8,128)(2,1)}), bf16[128,2048]{1,0:T(8,128)(2,1)}) %reduce-scatter.15.cloned.1.call-update) | async-done | bytes 524304 | tf_op jit(solution)/shard_map/reduce_scatter | solution.py:252
  716.8 36.1 %all-gather.21.cloned.1.call-done = bf16[1024,2048]{1,0:T(8,128)(2,1)} async-done(((bf16[128,2048]{1,0:T(8,128)(2,1)}), bf16[1024,2048]{1,0:T(8,128)(2,1)}) %all-gather.21.cloned.1.call-update) | async-done | bytes 4194320 | tf_op jit(solution)/shard_map/all_gather | solution.py:273
  770.8 14.8 %fusion.11 = f32[2048,2048]{1,0:T(8,128)} fusion(bf16[1024,2048]{1,0:T(8,128)(2,1)} %all-gather.13.cloned.1.call-done, bf16[1024,1024]{1,0:T(8,128)(2,1)} %copy-done.110, bf16[1024,1024]{1,0:T(8,128)(2,1)S(1)} %copy-done.109), kind=kOutput, calls=%fused_computation.26 | convolution fusion | flops 8598323200 | bytes 25165824 | tf_op jit(solution)/shard_map/dot_general | solution.py:22
  785.6 6.4 all-gather.19.cloned.1.call-done
  802.3 6.0 convolution_convert_fusion.1
  808.7 7.3 fusion
  816.0 6.2 add_convert_fusion.1
  822.2 16.9 %add_convert_fusion = bf16[2048,2048]{1,0:T(8,128)(2,1)} fusion(f32[2048,2048]{1,0:T(8,128)} %fusion.11, bf16[1024,2048]{1,0:T(8,128)(2,1)} %all-gather.17.cloned.1.call-done, bf16[1024,1024]{1,0:T(8,128)(2,1)} %copy-done.112, bf16[1024,1024]{1,0:T(8,128)(2,1)} %copy-done.111), kind=kOutput, calls=%fused_computation | convolution fusion | flops 8606711808 | bytes 33554432 | tf_op jit(solution)/shard_map/dot_general | solution.py:22
  854.4 12.8 psum.55
  867.9 34.8 %reduce-scatter.19.cloned.1.call-done = bf16[128,2048]{1,0:T(8,128)(2,1)} async-done(((bf16[1024,2048]{1,0:T(8,128)(2,1)}), bf16[128,2048]{1,0:T(8,128)(2,1)}) %reduce-scatter.19.cloned.1.call-update) | async-done | bytes 524304 | tf_op jit(solution)/shard_map/reduce_scatter | solution.py:301
  904.6 45.3 %all-reduce.6 = (f32[2048]{0:T(1024)}, f32[2048]{0:T(1024)}) all-reduce(f32[2048]{0:T(1024)S(1)} %add.352, f32[2048]{0:T(1024)S(1)} %add.353), channel_id=1, replica_groups=mesh['heads'=8,'batch'=4] {'heads','batch'}, use_global_device_ids=true, to_apply=%region_42.43 | all-reduce | flops 4096 | bytes 32768 | tf_op jit(solution)/shard_map/psum | solution.py:314
  953.6 449.8 %all-reduce.10.cloned.1.call-done = (bf16[2048,384]{1,0:T(8,128)(2,1)}, bf16[2048,2048]{1,0:T(8,128)(2,1)}, bf16[128,2048]{1,0:T(8,128)(2,1)}, bf16[1024,2048]{1,0:T(8,128)(2,1)}) async-done(((bf16[2048,384]{1,0:T(8,128)(2,1)}, bf16[2048,2048]{1,0:T(8,128)(2,1)}, bf16[128,2048]{1,0:T(8,128)(2,1)}, bf16[1024,2048]{1,0:T(8,128)(2,1)}), (bf16[2048,384]{1,0:T(8,128)(2,1)}, bf16[2048,2048]{1,0:T(8,128)(2,1)}, ...) | async-done | bytes 14680080 | tf_op jit(solution)/shard_map/psum | solution.py:308
  1403.4 11.9 fusion.155
  (383 shorter events, 125.2 us)
Async XLA Ops:
  7.2 55.9 %copy-start = (bf16[128,2048]{1,0:T(8,128)(2,1)S(1)}, bf16[128,2048]{1,0:T(8,128)(2,1)}, u32[]{:S(2)}) copy-start(bf16[128,2048]{1,0:T(8,128)(2,1)} %param.57) | copy-start | bytes 1572868
  7.2 44.3 %all-gather.15.cloned.1.call-start = ((), (), s32[]{:S(2)}) async-start(), calls=%async_computation.12 | async-start | bytes 4718592 | tf_op jit(solution)/shard_map/all_gather | solution.py:222
  12.0 78.8 %all-gather.11.cloned.1.call-start = ((), (), s32[]{:S(2)}) async-start(), calls=%async_computation.8 | async-start | bytes 4718592 | tf_op jit(solution)/shard_map/all_gather | solution.py:222
  12.8 153.4 %reduce-scatter.13.cloned.1.call-start = ((), (), s32[]{:S(2)}) async-start(), calls=%async_computation.13 | async-start | bytes 9437184 | tf_op jit(solution)/shard_map/reduce_scatter | solution.py:237
  13.8 44.4 %copy-start.98 = (pred[512]{0:T(512)(128)(4,1)}, pred[512]{0:T(512)(128)(4,1)S(1)}, u32[]{:S(2)}) copy-start(pred[512]{0:T(512)(128)(4,1)S(1)} %get-tuple-element.267) | copy-start | bytes 1540
  14.0 44.3 %copy-start.91 = (s32[512]{0:T(512)}, s32[512]{0:T(512)S(1)}, u32[]{:S(2)}) copy-start(s32[512]{0:T(512)S(1)} %get-tuple-element.330) | copy-start | bytes 6148
  14.0 44.3 %copy-start.93 = (s32[512]{0:T(512)}, s32[512]{0:T(512)S(1)}, u32[]{:S(2)}) copy-start(s32[512]{0:T(512)S(1)} %get-tuple-element.331) | copy-start | bytes 6148
  67.7 174.1 %reduce-scatter.9.cloned.1.call-start = ((), (), s32[]{:S(2)}) async-start(), calls=%async_computation.9 | async-start | bytes 9437184 | tf_op jit(solution)/shard_map/reduce_scatter | solution.py:237
  108.0 133.8 %copy-start.9 = (bf16[2,1,128,2048]{3,2,1,0:T(8,128)(2,1)S(1)}, bf16[2,1,128,2048]{3,2,1,0:T(8,128)(2,1)}, u32[]{:S(2)}) copy-start(bf16[2,1,128,2048]{3,2,1,0:T(8,128)(2,1)} %param.50) | copy-start | bytes 3145732
  108.0 136.6 %copy-start.63 = (f32[2048]{0:T(1024)S(1)}, f32[2048]{0:T(1024)}, u32[]{:S(2)}) copy-start(f32[2048]{0:T(1024)} %param.62) | copy-start | bytes 24580
  108.0 174.4 %all-gather.13.cloned.1.call-start = ((), (), s32[]{:S(2)}) async-start(), calls=%async_computation.10 | async-start | bytes 4718592 | tf_op jit(solution)/shard_map/all_gather | solution.py:246
  245.6 75.9 %all-gather.23.cloned.1.call-start = ((), (), s32[]{:S(2)}) async-start(), calls=%async_computation.22 | async-start | bytes 4718592 | tf_op jit(solution)/shard_map/all_gather | solution.py:260
  247.9 173.5 %reduce-scatter.17.cloned.1.call-start = ((), (), s32[]{:S(2)}) async-start(), calls=%async_computation.16 | async-start | bytes 9437184 | tf_op jit(solution)/shard_map/reduce_scatter | solution.py:267
  350.0 71.4 %copy-start.11 = (f32[128,2048]{1,0:T(8,128)S(1)}, f32[128,2048]{1,0:T(8,128)}, u32[]{:S(2)}) copy-start(f32[128,2048]{1,0:T(8,128)} %get-tuple-element.304) | copy-start | bytes 3145732
  350.0 111.3 %all-gather.17.cloned.1.call-start = ((), (), s32[]{:S(2)}) async-start(), calls=%async_computation.14 | async-start | bytes 4718592 | tf_op jit(solution)/shard_map/all_gather | solution.py:246
  424.5 76.2 %all-gather.25.cloned.1.call-start = ((), (), s32[]{:S(2)}) async-start(), calls=%async_computation.23 | async-start | bytes 4718592 | tf_op jit(solution)/shard_map/all_gather | solution.py:260
  425.2 175.6 %reduce-scatter.21.cloned.1.call-start = ((), (), s32[]{:S(2)}) async-start(), calls=%async_computation.19 | async-start | bytes 9437184 | tf_op jit(solution)/shard_map/reduce_scatter | solution.py:267
  529.3 126.7 %reduce-scatter.11.cloned.1.call-start = ((), (), s32[]{:S(2)}) async-start(), calls=%async_computation.11 | async-start | bytes 4718592 | tf_op jit(solution)/shard_map/reduce_scatter | solution.py:252
  539.5 172.0 %reduce-scatter.15.cloned.1.call-start = ((), (), s32[]{:S(2)}) async-start(), calls=%async_computation.15 | async-start | bytes 4718592 | tf_op jit(solution)/shard_map/reduce_scatter | solution.py:252
  550.0 202.9 %all-gather.21.cloned.1.call-start = ((), (), s32[]{:S(2)}) async-start(), calls=%async_computation.20 | async-start | bytes 4718592 | tf_op jit(solution)/shard_map/all_gather | solution.py:273
  716.1 75.9 %all-gather.19.cloned.1.call-start = ((), (), s32[]{:S(2)}) async-start(), calls=%async_computation.17 | async-start | bytes 4718592 | tf_op jit(solution)/shard_map/all_gather | solution.py:273
  716.7 41.6 %copy-start.15 = (bf16[1024,384]{0,1:T(8,128)(2,1)S(1)}, bf16[1024,384]{0,1:T(8,128)(2,1)}, u32[]{:S(2)}) copy-start(bf16[1024,384]{0,1:T(8,128)(2,1)} %copy-done.14) | copy-start | bytes 2359300
  716.7 41.6 %copy-start.86 = (f32[512]{0:T(512)S(1)}, f32[512]{0:T(512)}, u32[]{:S(2)}) copy-start(f32[512]{0:T(512)} %copy-done.85) | copy-start | bytes 6148
  716.8 41.6 %copy-start.92 = (s32[512]{0:T(512)S(1)}, s32[512]{0:T(512)}, u32[]{:S(2)}) copy-start(s32[512]{0:T(512)} %copy-done.91) | copy-start | bytes 6148
  716.8 151.1 %reduce-scatter.23.cloned.1.call-start = ((), (), s32[]{:S(2)}) async-start(), calls=%async_computation.21 | async-start | bytes 4718592 | tf_op jit(solution)/shard_map/reduce_scatter | solution.py:301
  769.2 133.5 %reduce-scatter.19.cloned.1.call-start = ((), (), s32[]{:S(2)}) async-start(), calls=%async_computation.18 | async-start | bytes 4718592 | tf_op jit(solution)/shard_map/reduce_scatter | solution.py:301
  808.4 595.0 %all-reduce.10.cloned.1.call-start = ((), (), s32[]{:S(2)}) async-start(), calls=%async_computation.24 | async-start | bytes 29360128 | tf_op jit(solution)/shard_map/psum | solution.py:308
  850.0 52.8 %copy-start.10 = (bf16[2,1,128,2048]{3,2,1,0:T(8,128)(2,1)S(1)}, bf16[2,1,128,2048]{3,2,1,0:T(8,128)(2,1)}, u32[]{:S(2)}) copy-start(bf16[2,1,128,2048]{3,2,1,0:T(8,128)(2,1)} %param.50) | copy-start | bytes 3145732
  850.0 52.8 %copy-start.64 = (f32[2048]{0:T(1024)S(1)}, f32[2048]{0:T(1024)}, u32[]{:S(2)}) copy-start(f32[2048]{0:T(1024)} %param.61) | copy-start | bytes 24580
  850.0 52.8 %copy-start.80 = (f32[128]{0:T(128)S(1)}, f32[128]{0:T(128)}, u32[]{:S(2)}) copy-start(f32[128]{0:T(128)} %copy-done.79) | copy-start | bytes 1540
  850.0 52.7 %copy-start.82 = (f32[128]{0:T(128)S(1)}, f32[128]{0:T(128)}, u32[]{:S(2)}) copy-start(f32[128]{0:T(128)} %copy-done.81) | copy-start | bytes 1540
  850.0 99.9 %copy-start.21 = (f32[128,2048]{1,0:T(8,128)S(1)}, f32[128,2048]{1,0:T(8,128)}, u32[]{:S(2)}) copy-start(f32[128,2048]{1,0:T(8,128)} %get-tuple-element.275) | copy-start | bytes 3145732
  (98 other events, 740.5 us)
Sparse Core Ops, SparseCore 0:
  12.1 39.4 all-gather.14
  54.1 36.7 all-gather.10
  94.8 71.3 reduce-scatter.12
  170.5 71.2 reduce-scatter.8
  245.7 36.6 all-gather.12
  284.8 36.7 all-gather.22
  350.2 71.2 reduce-scatter.16
  424.6 36.6 all-gather.16
  463.9 36.7 all-gather.24
  529.4 71.2 reduce-scatter.20
  604.7 51.3 reduce-scatter.10
  660.2 51.2 reduce-scatter.14
  716.2 36.6 all-gather.20
  755.3 36.7 all-gather.18
  795.8 51.3 reduce-scatter.22
  851.3 51.3 reduce-scatter.18
  906.6 496.7 all-reduce.9
where the time goes:
time: 1440 us; the launch traced here: 1430 us
  waiting for transfers between devices  1060 us (74%)
  matrix products  211 us (15%)
  blocking collectives  58.1 us (4%)
  local copies, waits for them, and re-layouts  42.1 us (3%)
  other arithmetic  34.4 us (2%)
  between operations  19.9 us (1%)
    psum x1, waiting for transfers between devices, per_device(): lax.psum(grad_qkv.astype(jnp.bfloat16), 'batch').astype(jnp.float32)  450 us
    reduce_scatter x2, waiting for transfers between devices, per_device(): lax.psum_scatter(jnp.dot(mixed_low, w_out, preferred_element_type=jnp.flo...  134 us
    reduce_scatter x2, waiting for transfers between devices, per_device(): lax.psum_scatter(dot_rows(d_gate_up, w_gate_up), 'heads', scatter_dimensi...  122 us
    reduce_scatter x2, waiting for transfers between devices, per_device(): lax.psum_scatter(jnp.dot(hidden, w_down, preferred_element_type=jnp.float...  109 us
    dot_general x20, matrix products, dot_rows(): lax.dot_general(left_mat, right_mat, (((1,), (1,)), ((), ())), preferred_...  79.7 us
    all_gather x2, waiting for transfers between devices, per_device(): full_mlp = lax.all_gather(low_mlp, 'heads', axis=0, tiled=True)  63.2 us
    all_gather x2, waiting for transfers between devices, per_device(): full_attn = lax.all_gather(low_attn, 'heads', axis=0, tiled=True)  57.5 us
    dot_general x20, matrix products, dot_cols(): lax.dot_general(left_mat, right_mat, (((0,), (0,)), ((), ())), preferred_...  57.2 us
  transfers between devices with their start and end apart: 17, of which 16 were waited for; matrix products, arithmetic and copies ran while one was open for 13% of the time, Pallas kernels for 0%

commit v1 on v0

--- a/solution.py
+++ b/solution.py
@@ -305,7 +305,7 @@
         grad_gain_attn = grad_gain_attn + gain_attn_part
         grad_in_list.append(d_x_norm + d_mid)
     grad_qkv, grad_out, grad_gate_up, grad_down, grad_mix = (
-        lax.psum(grad_qkv.astype(jnp.bfloat16), "batch").astype(jnp.float32),
+        jnp.sum(lax.all_gather(grad_qkv.astype(jnp.bfloat16), "batch"), axis=0).astype(jnp.float32),
         lax.psum(grad_out.astype(jnp.bfloat16), "batch").astype(jnp.float32),
         lax.psum(grad_gate_up.astype(jnp.bfloat16), "batch").astype(jnp.float32),
         lax.psum(grad_down.astype(jnp.bfloat16), "batch").astype(jnp.float32),

time: 1440 us -> 1500 us (1.042)
  waiting for transfers between devices: 1060 us -> 1120 us
    all_gather x0 -> x1, waiting for transfers between devices: none -> 63.6 us  [per_device(): lax.all_gather(grad_qkv.astype(jnp.bfloat16), 'batch')]
    all_gather x2, waiting for transfers between devices: 42.5 us -> 58.6 us  [per_device(): lax.all_gather(d_mid.astype(jnp.bfloat16), 'heads', axis=0, tiled=True)]
    reduce_scatter x2, waiting for transfers between devices: 34.8 us -> 18.9 us  [per_device(): lax.psum_scatter(dot_rows(d_qkv, w_qkv).astype(jnp.bfloat16), 'heads', sc...]
  transfers between devices with their start and end apart: 17 -> 18, of which waited for: 16 -> 17; matrix products, arithmetic and copies ran while one was open for 13% -> 13% of each run, Pallas kernels for 0% -> 0%
where the time goes in v1:
time: 1500 us; the launch traced here: 1490 us
  waiting for transfers between devices  1120 us (75%)
  matrix products  211 us (14%)
  blocking collectives  61.6 us (4%)
  local copies, waits for them, and re-layouts  41.1 us (3%)
  other arithmetic  39.2 us (3%)
  between operations  20 us (1%)
    psum x1, waiting for transfers between devices, per_device(): lax.psum(grad_gate_up.astype(jnp.bfloat16), 'batch').astype(jnp.float32)  439 us
    reduce_scatter x2, waiting for transfers between devices, per_device(): lax.psum_scatter(jnp.dot(mixed_low, w_out, preferred_element_type=jnp.flo...  134 us
    reduce_scatter x2, waiting for transfers between devices, per_device(): lax.psum_scatter(dot_rows(d_gate_up, w_gate_up), 'heads', scatter_dimensi...  122 us
    reduce_scatter x2, waiting for transfers between devices, per_device(): lax.psum_scatter(jnp.dot(hidden, w_down, preferred_element_type=jnp.float...  109 us
    dot_general x20, matrix products, dot_rows(): lax.dot_general(left_mat, right_mat, (((1,), (1,)), ((), ())), preferred_...  79.7 us
    all_gather x1, waiting for transfers between devices, per_device(): lax.all_gather(grad_qkv.astype(jnp.bfloat16), 'batch')  63.6 us
    all_gather x2, waiting for transfers between devices, per_device(): full_mlp = lax.all_gather(low_mlp, 'heads', axis=0, tiled=True)  63.2 us
    all_gather x2, waiting for transfers between devices, per_device(): lax.all_gather(d_mid.astype(jnp.bfloat16), 'heads', axis=0, tiled=True)  58.6 us
  transfers between devices with their start and end apart: 18, of which 17 were waited for; matrix products, arithmetic and copies ran while one was open for 13% of the time, Pallas kernels for 0%

profile of v1, /device:TPU:0, one launch (start us, length us, event | category | flops | bytes accessed | tf_op | source)
XLA Modules:
  0.0 1492.1 jit_solution(10714820369222798011)
XLA Ops:
  16.6 34.9 %all-gather.17.cloned.1.call-done = bf16[1024,2048]{1,0:T(8,128)(2,1)} async-done(((bf16[128,2048]{1,0:T(8,128)(2,1)}), bf16[1024,2048]{1,0:T(8,128)(2,1)}) %all-gather.17.cloned.1.call-update) | async-done | bytes 4194320 | tf_op jit(solution)/shard_map/all_gather | solution.py:222
  68.3 22.4 %all-gather.13.cloned.1.call-done = bf16[1024,2048]{1,0:T(8,128)(2,1)} async-done(((bf16[128,2048]{1,0:T(8,128)(2,1)}), bf16[1024,2048]{1,0:T(8,128)(2,1)}) %all-gather.13.cloned.1.call-update) | async-done | bytes 4194320 | tf_op jit(solution)/shard_map/all_gather | solution.py:222
  108.0 58.2 %reduce-scatter.13.cloned.1.call-done = f32[128,2048]{1,0:T(8,128)} async-done(((f32[1024,2048]{1,0:T(8,128)}), f32[128,2048]{1,0:T(8,128)}) %reduce-scatter.13.cloned.1.call-update) | async-done | bytes 1048592 | tf_op jit(solution)/shard_map/reduce_scatter | solution.py:237
  166.2 75.6 %reduce-scatter.9.cloned.1.call-done = f32[128,2048]{1,0:T(8,128)} async-done(((f32[1024,2048]{1,0:T(8,128)}), f32[128,2048]{1,0:T(8,128)}) %reduce-scatter.9.cloned.1.call-update) | async-done | bytes 1048592 | tf_op jit(solution)/shard_map/reduce_scatter | solution.py:237
  255.2 27.2 %all-gather.15.cloned.1.call-done = bf16[1024,2048]{1,0:T(8,128)(2,1)} async-done(((bf16[128,2048]{1,0:T(8,128)(2,1)}), bf16[1024,2048]{1,0:T(8,128)(2,1)}) %all-gather.15.cloned.1.call-update) | async-done | bytes 4194320 | tf_op jit(solution)/shard_map/all_gather | solution.py:246
  282.4 15.0 %fusion.167 = f32[1024,2048]{1,0:T(8,128)} fusion(bf16[1024,2048]{1,0:T(8,128)(2,1)} %all-gather.15.cloned.1.call-done, bf16[2048,2048]{1,0:T(8,128)(2,1)} %constant_dynamic-update-slice_fusion.3), kind=kOutput, calls=%fused_computation.320 | convolution fusion | flops 8589934592 | bytes 20971520 | tf_op jit(solution)/shard_map/dot_general | solution.py:247
  297.4 24.1 %all-gather.25.cloned.1.call-done = bf16[1,1,1024,2048]{3,2,1,0:T(8,128)(2,1)} async-done(((bf16[1,1,128,2048]{3,2,1,0:T(8,128)(2,1)}), bf16[1,1,1024,2048]{3,2,1,0:T(8,128)(2,1)}) %all-gather.25.cloned.1.call-update) | async-done | bytes 4194320 | tf_op jit(solution)/shard_map/all_gather | solution.py:260
  321.5 13.2 multiply_convert_fusion.3
  336.8 13.3 fusion.12
  350.1 71.3 %reduce-scatter.17.cloned.1.call-done = f32[128,2048]{1,0:T(8,128)} async-done(((f32[1024,2048]{1,0:T(8,128)}), f32[128,2048]{1,0:T(8,128)}) %reduce-scatter.17.cloned.1.call-update) | async-done | bytes 1048592 | tf_op jit(solution)/shard_map/reduce_scatter | solution.py:267
  425.3 36.1 %all-gather.19.cloned.1.call-done = bf16[1024,2048]{1,0:T(8,128)(2,1)} async-done(((bf16[128,2048]{1,0:T(8,128)(2,1)}), bf16[1024,2048]{1,0:T(8,128)(2,1)}) %all-gather.19.cloned.1.call-update) | async-done | bytes 4194320 | tf_op jit(solution)/shard_map/all_gather | solution.py:246
  461.4 14.6 fusion.169
  476.0 24.7 %all-gather.27.cloned.1.call-done = bf16[1,1,1024,2048]{3,2,1,0:T(8,128)(2,1)} async-done(((bf16[1,1,128,2048]{3,2,1,0:T(8,128)(2,1)}), bf16[1,1,1024,2048]{3,2,1,0:T(8,128)(2,1)}) %all-gather.27.cloned.1.call-update) | async-done | bytes 4194320 | tf_op jit(solution)/shard_map/all_gather | solution.py:260
  500.7 13.2 multiply_convert_fusion.1
  516.0 13.3 fusion.10
  529.7 9.7 convolution_convert_fusion.3
  539.5 10.4 convolution_convert_fusion.2
  550.0 50.7 %reduce-scatter.21.cloned.1.call-done = f32[128,2048]{1,0:T(8,128)} async-done(((f32[1024,2048]{1,0:T(8,128)}), f32[128,2048]{1,0:T(8,128)}) %reduce-scatter.21.cloned.1.call-update) | async-done | bytes 1048592 | tf_op jit(solution)/shard_map/reduce_scatter | solution.py:267
  602.2 53.8 %reduce-scatter.11.cloned.1.call-done = bf16[128,2048]{1,0:T(8,128)(2,1)} async-done(((bf16[1024,2048]{1,0:T(8,128)(2,1)}), bf16[128,2048]{1,0:T(8,128)(2,1)}) %reduce-scatter.11.cloned.1.call-update) | async-done | bytes 524304 | tf_op jit(solution)/shard_map/reduce_scatter | solution.py:252
  656.0 55.5 %reduce-scatter.15.cloned.1.call-done = bf16[128,2048]{1,0:T(8,128)(2,1)} async-done(((bf16[1024,2048]{1,0:T(8,128)(2,1)}), bf16[128,2048]{1,0:T(8,128)(2,1)}) %reduce-scatter.15.cloned.1.call-update) | async-done | bytes 524304 | tf_op jit(solution)/shard_map/reduce_scatter | solution.py:252
  716.8 36.1 %all-gather.23.cloned.1.call-done = bf16[1024,2048]{1,0:T(8,128)(2,1)} async-done(((bf16[128,2048]{1,0:T(8,128)(2,1)}), bf16[1024,2048]{1,0:T(8,128)(2,1)}) %all-gather.23.cloned.1.call-update) | async-done | bytes 4194320 | tf_op jit(solution)/shard_map/all_gather | solution.py:273
  769.5 22.5 %all-gather.21.cloned.1.call-done = bf16[1024,2048]{1,0:T(8,128)(2,1)} async-done(((bf16[128,2048]{1,0:T(8,128)(2,1)}), bf16[1024,2048]{1,0:T(8,128)(2,1)}) %all-gather.21.cloned.1.call-update) | async-done | bytes 4194320 | tf_op jit(solution)/shard_map/all_gather | solution.py:273
  802.3 6.0 convolution_convert_fusion.1
  818.0 15.8 %fusion.11 = f32[2048,2048]{1,0:T(8,128)} fusion(bf16[1024,2048]{1,0:T(8,128)(2,1)} %all-gather.15.cloned.1.call-done, bf16[1024,1024]{1,0:T(8,128)(2,1)} %copy-done.109, bf16[1024,1024]{1,0:T(8,128)(2,1)} %copy-done.108), kind=kOutput, calls=%fused_computation.26 | convolution fusion | flops 8598323200 | bytes 25165824 | tf_op jit(solution)/shard_map/dot_general | solution.py:22
  838.5 6.2 add_convert_fusion.1
  844.6 16.8 %add_convert_fusion = bf16[2048,2048]{1,0:T(8,128)(2,1)} fusion(f32[2048,2048]{1,0:T(8,128)} %fusion.11, bf16[1024,2048]{1,0:T(8,128)(2,1)} %all-gather.19.cloned.1.call-done, bf16[1024,1024]{1,0:T(8,128)(2,1)} %copy-done.112, bf16[1024,1024]{1,0:T(8,128)(2,1)S(1)} %copy-done.111), kind=kOutput, calls=%fused_computation | convolution fusion | flops 8606711808 | bytes 33554432 | tf_op jit(solution)/shard_map/dot_general | solution.py:22
  870.1 13.1 psum.47
  883.9 18.8 %reduce-scatter.19.cloned.1.call-done = bf16[128,2048]{1,0:T(8,128)(2,1)} async-done(((bf16[1024,2048]{1,0:T(8,128)(2,1)}), bf16[128,2048]{1,0:T(8,128)(2,1)}) %reduce-scatter.19.cloned.1.call-update) | async-done | bytes 524304 | tf_op jit(solution)/shard_map/reduce_scatter | solution.py:301
  904.6 48.5 %all-reduce.6 = (f32[2048]{0:T(1024)}, f32[2048]{0:T(1024)}) all-reduce(f32[2048]{0:T(1024)S(1)} %add.350, f32[2048]{0:T(1024)S(1)} %add.351), channel_id=1, replica_groups=mesh['heads'=8,'batch'=4] {'heads','batch'}, use_global_device_ids=true, to_apply=%region_42.43 | all-reduce | flops 4096 | bytes 32768 | tf_op jit(solution)/shard_map/psum | solution.py:314
  956.9 63.6 %all-gather.29.cloned.1.call-done = bf16[8192,384]{1,0:T(8,128)(2,1)} async-done(((bf16[2048,384]{1,0:T(8,128)(2,1)}), bf16[8192,384]{1,0:T(8,128)(2,1)}) %all-gather.29.cloned.1.call-update) | async-done | bytes 6291472 | tf_op jit(solution)/shard_map/all_gather | solution.py:308
  1027.0 439.4 %all-reduce.10.cloned.1.call-done = (bf16[2048,2048]{1,0:T(8,128)(2,1)}, bf16[128,2048]{1,0:T(8,128)(2,1)}, bf16[1024,2048]{1,0:T(8,128)(2,1)}) async-done(((bf16[2048,2048]{1,0:T(8,128)(2,1)}, bf16[128,2048]{1,0:T(8,128)(2,1)}, bf16[1024,2048]{1,0:T(8,128)(2,1)}), (bf16[2048,2048]{1,0:T(8,128)(2,1)}, bf16[128,2048]{1,0:T(8,128)(2,1)}, bf16[1024,2048]{1,0:T(8,128)(2,1)})) %all-reduce.10.cloned.1.call-update) | async-done | bytes 13107216 | tf_op jit(solution)/shard_map/psum | solution.py:310
  1466.5 11.9 fusion.155
  (387 shorter events, 136.0 us)
Async XLA Ops:
  7.2 55.8 %copy-start = (bf16[128,2048]{1,0:T(8,128)(2,1)S(1)}, bf16[128,2048]{1,0:T(8,128)(2,1)}, u32[]{:S(2)}) copy-start(bf16[128,2048]{1,0:T(8,128)(2,1)} %param.57) | copy-start | bytes 1572868
  7.2 44.3 %all-gather.17.cloned.1.call-start = ((), (), s32[]{:S(2)}) async-start(), calls=%async_computation.12 | async-start | bytes 4718592 | tf_op jit(solution)/shard_map/all_gather | solution.py:222
  12.0 78.8 %all-gather.13.cloned.1.call-start = ((), (), s32[]{:S(2)}) async-start(), calls=%async_computation.8 | async-start | bytes 4718592 | tf_op jit(solution)/shard_map/all_gather | solution.py:222
  12.7 153.4 %reduce-scatter.13.cloned.1.call-start = ((), (), s32[]{:S(2)}) async-start(), calls=%async_computation.13 | async-start | bytes 9437184 | tf_op jit(solution)/shard_map/reduce_scatter | solution.py:237
  13.8 44.4 %copy-start.97 = (pred[512]{0:T(512)(128)(4,1)}, pred[512]{0:T(512)(128)(4,1)S(1)}, u32[]{:S(2)}) copy-start(pred[512]{0:T(512)(128)(4,1)S(1)} %get-tuple-element.267) | copy-start | bytes 1540
  13.9 44.3 %copy-start.90 = (s32[512]{0:T(512)}, s32[512]{0:T(512)S(1)}, u32[]{:S(2)}) copy-start(s32[512]{0:T(512)S(1)} %get-tuple-element.329) | copy-start | bytes 6148
  13.9 44.3 %copy-start.92 = (s32[512]{0:T(512)}, s32[512]{0:T(512)S(1)}, u32[]{:S(2)}) copy-start(s32[512]{0:T(512)S(1)} %get-tuple-element.330) | copy-start | bytes 6148
  67.7 174.1 %reduce-scatter.9.cloned.1.call-start = ((), (), s32[]{:S(2)}) async-start(), calls=%async_computation.9 | async-start | bytes 9437184 | tf_op jit(solution)/shard_map/reduce_scatter | solution.py:237
  107.9 133.9 %copy-start.9 = (bf16[2,1,128,2048]{3,2,1,0:T(8,128)(2,1)S(1)}, bf16[2,1,128,2048]{3,2,1,0:T(8,128)(2,1)}, u32[]{:S(2)}) copy-start(bf16[2,1,128,2048]{3,2,1,0:T(8,128)(2,1)} %param.50) | copy-start | bytes 3145732
  108.0 136.6 %copy-start.62 = (f32[2048]{0:T(1024)S(1)}, f32[2048]{0:T(1024)}, u32[]{:S(2)}) copy-start(f32[2048]{0:T(1024)} %param.62) | copy-start | bytes 24580
  108.0 174.4 %all-gather.15.cloned.1.call-start = ((), (), s32[]{:S(2)}) async-start(), calls=%async_computation.10 | async-start | bytes 4718592 | tf_op jit(solution)/shard_map/all_gather | solution.py:246
  245.6 75.9 %all-gather.25.cloned.1.call-start = ((), (), s32[]{:S(2)}) async-start(), calls=%async_computation.22 | async-start | bytes 4718592 | tf_op jit(solution)/shard_map/all_gather | solution.py:260
  247.9 173.6 %reduce-scatter.17.cloned.1.call-start = ((), (), s32[]{:S(2)}) async-start(), calls=%async_computation.16 | async-start | bytes 9437184 | tf_op jit(solution)/shard_map/reduce_scatter | solution.py:267
  350.1 71.4 %copy-start.11 = (f32[128,2048]{1,0:T(8,128)S(1)}, f32[128,2048]{1,0:T(8,128)}, u32[]{:S(2)}) copy-start(f32[128,2048]{1,0:T(8,128)} %get-tuple-element.303) | copy-start | bytes 3145732
  350.1 111.3 %all-gather.19.cloned.1.call-start = ((), (), s32[]{:S(2)}) async-start(), calls=%async_computation.14 | async-start | bytes 4718592 | tf_op jit(solution)/shard_map/all_gather | solution.py:246
  424.5 76.2 %all-gather.27.cloned.1.call-start = ((), (), s32[]{:S(2)}) async-start(), calls=%async_computation.23 | async-start | bytes 4718592 | tf_op jit(solution)/shard_map/all_gather | solution.py:260
  425.2 175.5 %reduce-scatter.21.cloned.1.call-start = ((), (), s32[]{:S(2)}) async-start(), calls=%async_computation.19 | async-start | bytes 9437184 | tf_op jit(solution)/shard_map/reduce_scatter | solution.py:267
  529.3 126.7 %reduce-scatter.11.cloned.1.call-start = ((), (), s32[]{:S(2)}) async-start(), calls=%async_computation.11 | async-start | bytes 4718592 | tf_op jit(solution)/shard_map/reduce_scatter | solution.py:252
  539.5 172.0 %reduce-scatter.15.cloned.1.call-start = ((), (), s32[]{:S(2)}) async-start(), calls=%async_computation.15 | async-start | bytes 4718592 | tf_op jit(solution)/shard_map/reduce_scatter | solution.py:252
  550.0 203.0 %all-gather.23.cloned.1.call-start = ((), (), s32[]{:S(2)}) async-start(), calls=%async_computation.20 | async-start | bytes 4718592 | tf_op jit(solution)/shard_map/all_gather | solution.py:273
  716.1 75.9 %all-gather.21.cloned.1.call-start = ((), (), s32[]{:S(2)}) async-start(), calls=%async_computation.17 | async-start | bytes 4718592 | tf_op jit(solution)/shard_map/all_gather | solution.py:273
  716.7 41.6 %copy-start.76 = (f32[512]{0:T(512)S(1)}, f32[512]{0:T(512)}, u32[]{:S(2)}) copy-start(f32[512]{0:T(512)} %copy-done.75) | copy-start | bytes 6148
  716.7 41.6 %copy-start.15 = (bf16[1024,384]{0,1:T(8,128)(2,1)S(1)}, bf16[1024,384]{0,1:T(8,128)(2,1)}, u32[]{:S(2)}) copy-start(bf16[1024,384]{0,1:T(8,128)(2,1)} %copy-done.14) | copy-start | bytes 2359300
  716.7 41.6 %copy-start.85 = (f32[512]{0:T(512)S(1)}, f32[512]{0:T(512)}, u32[]{:S(2)}) copy-start(f32[512]{0:T(512)} %copy-done.84) | copy-start | bytes 6148
  716.7 41.6 %copy-start.91 = (s32[512]{0:T(512)S(1)}, s32[512]{0:T(512)}, u32[]{:S(2)}) copy-start(s32[512]{0:T(512)} %copy-done.90) | copy-start | bytes 6148
  716.8 41.6 %copy-start.93 = (s32[512]{0:T(512)S(1)}, s32[512]{0:T(512)}, u32[]{:S(2)}) copy-start(s32[512]{0:T(512)} %copy-done.92) | copy-start | bytes 6148
  716.8 41.6 %copy-start.98 = (pred[512]{0:T(512)(128)(4,1)S(1)}, pred[512]{0:T(512)(128)(4,1)}, u32[]{:S(2)}) copy-start(pred[512]{0:T(512)(128)(4,1)} %copy-done.97) | copy-start | bytes 1540
  716.8 167.1 %reduce-scatter.23.cloned.1.call-start = ((), (), s32[]{:S(2)}) async-start(), calls=%async_computation.21 | async-start | bytes 4718592 | tf_op jit(solution)/shard_map/reduce_scatter | solution.py:301
  769.3 133.4 %reduce-scatter.19.cloned.1.call-start = ((), (), s32[]{:S(2)}) async-start(), calls=%async_computation.18 | async-start | bytes 4718592 | tf_op jit(solution)/shard_map/reduce_scatter | solution.py:301
  808.3 212.2 %all-gather.29.cloned.1.call-start = ((), (), s32[]{:S(2)}) async-start(), calls=%async_computation.24 | async-start | bytes 7864320 | tf_op jit(solution)/shard_map/all_gather | solution.py:308
  817.7 648.7 %all-reduce.10.cloned.1.call-start = ((), (), s32[]{:S(2)}) async-start(), calls=%async_computation.25 | async-start | bytes 26214400 | tf_op jit(solution)/shard_map/psum | solution.py:310
  865.7 87.4 %copy-start.20 = (f32[128,2048]{1,0:T(8,128)S(1)}, f32[128,2048]{1,0:T(8,128)}, u32[]{:S(2)}) copy-start(f32[128,2048]{1,0:T(8,128)} %get-tuple-element.274) | copy-start | bytes 3145732
  (99 other events, 965.5 us)
Sparse Core Ops, SparseCore 0:
  12.1 39.4 all-gather.16
  54.0 36.7 all-gather.12
  94.8 71.3 reduce-scatter.12
  170.5 71.2 reduce-scatter.8
  245.7 36.6 all-gather.14
  284.7 36.7 all-gather.24
  350.2 71.2 reduce-scatter.16
  424.6 36.6 all-gather.18
  464.0 36.7 all-gather.26
  529.4 71.2 reduce-scatter.20
  604.6 51.3 reduce-scatter.10
  660.2 51.3 reduce-scatter.14
  716.2 36.6 all-gather.22
  755.3 36.7 all-gather.20
  795.8 51.3 reduce-scatter.22
  851.3 51.3 reduce-scatter.18
  904.1 116.3 all-gather.28
  1023.8 442.6 all-reduce.9
